TPU v7x, 32 devices: a whole 2x2x4 slice. The times are simulated.
32 devices in a mesh: rep: 2 (over x), shard: 16 (over z, y, core).
Axes of the slice: x: 2, y: 2, z: 4, core: 2. Of those that a mesh axis runs over, the one named last changes fastest.
Arguments:
- tokens: bfloat16 [4096, 1024], P(('rep', 'shard')), may hold values from -6 to 6
- cotangent: bfloat16 [4096, 1024], P(('rep', 'shard')), may hold values from -6 to 6
- segment: int32 [4096], P(('rep', 'shard')), may hold values from -1 to 127, as said below
- params: float32 [12596224], P('shard'), as said below
- first_moment: float32 [12596224], P('shard'), may hold values from -6 to 6
- second_moment: float32 [12596224], P('shard'), may hold values from 0.01 to 1
Outputs:
- output_rows: bfloat16 [4096, 1024], P(('rep', 'shard'))
- input_grad: bfloat16 [4096, 1024], P(('rep', 'shard'))
- param_grad: float32 [12596224], P('shard')
- new_params: float32 [12596224], P('shard')
- new_first: float32 [12596224], P('shard')
- new_second: float32 [12596224], P('shard')
Inputs may be any that keep to these rules, and one draw needn't show every extreme that they name: `segment`: within each aligned block of 128 rows (the rows of one device) the occupied slots come first; an occupied slot holds the index within the block of the first slot of its sequence, so the first slot holds 0 and values never fall along the occupied slots; empty slots hold -1. `params`: the flat buffer in the layout of the steps.
All inputs are finite; a program needn't handle non-finite values.
Results may differ from a plain program's by a relative error of at most 0.023.
Values may be sent and summed in bfloat16 or wider, within the bound.
No kernel may reach another device: no remote copies, remote signals or barrier semaphores. Data moves between devices by JAX's collectives and lax.ppermute only.
A program may use at most 192 MiB of HBM per device.

v0:
```python
import math
import jax
import jax.numpy as jnp
from jax import lax
from jax.sharding import PartitionSpec as P

D = 1024
HEADS = 16
HD = 64
ROT = 16
FF = 4096
STEP = 4
norm_eps = 1e-05
adam_eps = 1e-08
beta_one = 0.9
beta_two = 0.999
learn_rate = 0.003
decay_rate = 0.1
root_half = 0.7071067811865476
inv_root_twopi = 0.3989422804014327


def extent_list():
    return [
        (D, 3 * D),
        (3 * D,),
        (D, D),
        (D,),
        (D, FF),
        (FF,),
        (FF, D),
        (D,),
        (D,),
        (D,),
        (D,),
        (D,),
    ]


def unpack(flat_vec):
    pieces = []
    offset = 0
    for extent in extent_list():
        amount = math.prod(extent)
        pieces.append(flat_vec[offset : offset + amount].reshape(extent))
        offset += amount
    return pieces


def norm_forward(residual, gain, shift):
    center = residual - jnp.mean(residual, axis=-1, keepdims=True)
    inverse = lax.rsqrt(jnp.mean(center * center, axis=-1, keepdims=True) + norm_eps)
    normed = center * inverse
    return (normed * gain + shift, normed, inverse)


def norm_backward(grad_norm, normed, inverse, gain):
    grad_hat = grad_norm * gain
    return inverse * (
        grad_hat
        - jnp.mean(grad_hat, axis=-1, keepdims=True)
        - normed * jnp.mean(grad_hat * normed, axis=-1, keepdims=True)
    )


def rotate(values, cosine, sine_part):
    half_rot = ROT // 2
    lower_half = values[..., :half_rot]
    upper_half = values[..., half_rot:ROT]
    return jnp.concatenate(
        [
            lower_half * cosine - upper_half * sine_part,
            upper_half * cosine + lower_half * sine_part,
            values[..., ROT:],
        ],
        axis=-1,
    )


def rotate_back(grads_in, cosine, sine_part):
    half_rot = ROT // 2
    lower_half = grads_in[..., :half_rot]
    upper_half = grads_in[..., half_rot:ROT]
    return jnp.concatenate(
        [
            lower_half * cosine + upper_half * sine_part,
            upper_half * cosine - lower_half * sine_part,
            grads_in[..., ROT:],
        ],
        axis=-1,
    )


def gelu_exact(values):
    return 0.5 * values * (1.0 + lax.erf(values * root_half))


def gelu_slope(values):
    return (
        0.5 * (1.0 + lax.erf(values * root_half))
        + values * jnp.exp(-0.5 * values * values) * inv_root_twopi
    )


def angles(segments):
    row_ids = jnp.arange(segments.shape[0], dtype=jnp.int32)
    position = (row_ids - segments).astype(jnp.float32)
    frequency = 10000.0 ** (-jnp.arange(0, ROT, 2, dtype=jnp.float32) / ROT)
    phases = position[:, None] * frequency[None, :]
    return (jnp.cos(phases)[:, None, :], jnp.sin(phases)[:, None, :])


def scores_of(queries, keys_bf, segments):
    raw = jnp.einsum("ihd,jhd->hij", queries, keys_bf, preferred_element_type=jnp.float32) * HD ** (
        -0.5
    )
    row_ids = jnp.arange(segments.shape[0], dtype=jnp.int32)
    allowed = (segments[:, None] == segments[None, :]) & (row_ids[None, :] <= row_ids[:, None])
    return jnp.where(allowed[None], raw, -1e30)


def layer_block(rows_in, rows_cot, segments, pieces):
    (
        w_qkv,
        b_qkv,
        w_out,
        b_out,
        w_up,
        b_up,
        w_down,
        b_down,
        gain_one,
        shift_one,
        gain_two,
        shift_two,
    ) = pieces
    length = rows_in.shape[0]
    residual = rows_in.astype(jnp.float32)
    normed_one, hat_one, inv_one = norm_forward(
        residual, gain_one.astype(jnp.float32), shift_one.astype(jnp.float32)
    )
    normed_two, hat_two, inv_two = norm_forward(
        residual, gain_two.astype(jnp.float32), shift_two.astype(jnp.float32)
    )
    input_one = normed_one.astype(jnp.bfloat16)
    input_two = normed_two.astype(jnp.bfloat16)
    mixed_rows = jnp.dot(input_one, w_qkv, preferred_element_type=jnp.float32) + b_qkv.astype(
        jnp.float32
    )
    cosine, sine_part = angles(segments)
    queries = rotate(mixed_rows[:, :D].reshape(length, HEADS, HD), cosine, sine_part).astype(
        jnp.bfloat16
    )
    keys_bf = rotate(mixed_rows[:, D : 2 * D].reshape(length, HEADS, HD), cosine, sine_part).astype(
        jnp.bfloat16
    )
    values_bf = mixed_rows[:, 2 * D :].reshape(length, HEADS, HD).astype(jnp.bfloat16)
    scores = scores_of(queries, keys_bf, segments)
    row_max = jnp.max(scores, axis=-1, keepdims=True)
    log_total = row_max + jnp.log(jnp.sum(jnp.exp(scores - row_max), axis=-1, keepdims=True))
    probs_bf = jnp.exp(scores - log_total).astype(jnp.bfloat16)
    heads_out = (
        jnp.einsum("hij,jhd->ihd", probs_bf, values_bf, preferred_element_type=jnp.float32)
        .reshape(length, D)
        .astype(jnp.bfloat16)
    )
    attention = jnp.dot(heads_out, w_out, preferred_element_type=jnp.float32) + b_out.astype(
        jnp.float32
    )
    hidden_pre = jnp.dot(input_two, w_up, preferred_element_type=jnp.float32) + b_up.astype(
        jnp.float32
    )
    active = gelu_exact(hidden_pre).astype(jnp.bfloat16)
    feed_out = jnp.dot(active, w_down, preferred_element_type=jnp.float32) + b_down.astype(
        jnp.float32
    )
    out_rows = (residual + attention + feed_out).astype(jnp.bfloat16)
    live_rows = (segments >= 0)[:, None]
    grad_bf = jnp.where(live_rows, rows_cot, jnp.zeros_like(rows_cot))
    grad_full = grad_bf.astype(jnp.float32)
    grad_w_down = jnp.dot(active.T, grad_bf, preferred_element_type=jnp.float32)
    grad_b_down = jnp.sum(grad_full, axis=0)
    grad_hidden = jnp.dot(grad_bf, w_down.T, preferred_element_type=jnp.float32) * gelu_slope(
        hidden_pre
    )
    grad_hidden_bf = grad_hidden.astype(jnp.bfloat16)
    grad_b_up = jnp.sum(grad_hidden, axis=0)
    grad_w_up = jnp.dot(input_two.T, grad_hidden_bf, preferred_element_type=jnp.float32)
    grad_norm_two = jnp.dot(grad_hidden_bf, w_up.T, preferred_element_type=jnp.float32)
    grad_w_out = jnp.dot(heads_out.T, grad_bf, preferred_element_type=jnp.float32)
    grad_heads = (
        jnp.dot(grad_bf, w_out.T, preferred_element_type=jnp.float32)
        .astype(jnp.bfloat16)
        .reshape(length, HEADS, HD)
    )
    delta_rows = jnp.einsum(
        "ihd,ihd->hi",
        grad_heads.astype(jnp.float32),
        heads_out.reshape(length, HEADS, HD).astype(jnp.float32),
    )
    probs_exact = jnp.exp(scores_of(queries, keys_bf, segments) - log_total)
    probs_again = probs_exact.astype(jnp.bfloat16)
    grad_values = jnp.einsum(
        "hij,ihd->jhd", probs_again, grad_heads, preferred_element_type=jnp.float32
    )
    grad_probs = jnp.einsum(
        "ihd,jhd->hij", grad_heads, values_bf, preferred_element_type=jnp.float32
    )
    grad_scores = (probs_exact * (grad_probs - delta_rows[:, :, None]) * HD ** (-0.5)).astype(
        jnp.bfloat16
    )
    grad_queries = jnp.einsum(
        "hij,jhd->ihd", grad_scores, keys_bf, preferred_element_type=jnp.float32
    )
    grad_keys = jnp.einsum("hij,ihd->jhd", grad_scores, queries, preferred_element_type=jnp.float32)
    grad_mixed = jnp.concatenate(
        [
            rotate_back(grad_queries, cosine, sine_part).reshape(length, D),
            rotate_back(grad_keys, cosine, sine_part).reshape(length, D),
            grad_values.reshape(length, D),
        ],
        axis=1,
    )
    grad_b_qkv = jnp.sum(grad_mixed, axis=0)
    grad_mixed_bf = grad_mixed.astype(jnp.bfloat16)
    grad_w_qkv = jnp.dot(input_one.T, grad_mixed_bf, preferred_element_type=jnp.float32)
    grad_norm_one = jnp.dot(grad_mixed_bf, w_qkv.T, preferred_element_type=jnp.float32)
    grad_rows = (
        grad_full
        + norm_backward(grad_norm_one, hat_one, inv_one, gain_one.astype(jnp.float32))
        + norm_backward(grad_norm_two, hat_two, inv_two, gain_two.astype(jnp.float32))
    ).astype(jnp.bfloat16)
    grad_list = [
        grad_w_qkv,
        grad_b_qkv,
        grad_w_out,
        grad_b_down,
        grad_w_up,
        grad_b_up,
        grad_w_down,
        grad_b_down,
        jnp.sum(grad_norm_one * hat_one, axis=0),
        jnp.sum(grad_norm_one, axis=0),
        jnp.sum(grad_norm_two * hat_two, axis=0),
        jnp.sum(grad_norm_two, axis=0),
    ]
    block_grad = jnp.concatenate([piece.reshape(-1).astype(jnp.bfloat16) for piece in grad_list])
    return (out_rows, grad_rows, block_grad)


def adam_update(weights, moment_one, moment_two, grad_total):
    first_new = beta_one * moment_one + (1.0 - beta_one) * grad_total
    second_new = beta_two * moment_two + (1.0 - beta_two) * grad_total * grad_total
    correct_one = 1.0 - beta_one**STEP
    correct_two = 1.0 - beta_two**STEP
    change = first_new / correct_one / (jnp.sqrt(second_new / correct_two) + adam_eps)
    return (weights - learn_rate * (change + decay_rate * weights), first_new, second_new)


def per_device(tokens, cotangent, segment, params, first_moment, second_moment):
    gathered = lax.all_gather(params.astype(jnp.bfloat16), "shard", axis=0, tiled=True)
    pieces = unpack(gathered)
    out_rows, grad_rows, block_grad = layer_block(tokens, cotangent, segment, pieces)
    owner_part = lax.psum_scatter(
        block_grad.astype(jnp.float32).astype(jnp.bfloat16),
        "shard",
        scatter_dimension=0,
        tiled=True,
    )
    grad_total = lax.psum(owner_part, "rep").astype(jnp.float32)
    new_weights, first_new, second_new = adam_update(
        params, first_moment, second_moment, grad_total
    )
    return (out_rows, grad_rows, grad_total, new_weights, first_new, second_new)


def solution(mesh):
    in_specs = (
        P(("rep", "shard"), None),
        P(("rep", "shard"), None),
        P(("rep", "shard")),
        P("shard"),
        P("shard"),
        P("shard"),
    )
    out_specs = (
        P(("rep", "shard"), None),
        P(("rep", "shard"), None),
        P("shard"),
        P("shard"),
        P("shard"),
        P("shard"),
    )
    return jax.shard_map(
        per_device, mesh=mesh, in_specs=in_specs, out_specs=out_specs, check_vma=False
    )
```

profile of v0, /device:TPU:0, one launch (start us, length us, event | category | flops | bytes accessed | tf_op | source)
XLA Modules:
  0.0 1133.9 jit_solution(3433474658904389262)
XLA Ops:
  7.2 2.0 convert_element_type.138
  9.3 0.6 fusion.63
  10.6 8.5 broadcast.159
  19.0 24.7 %dynamic-update-slice = bf16[12596224]{0:T(1024)(128)(2,1)} dynamic-update-slice(bf16[12596224]{0:T(1024)(128)(2,1)} %broadcast.159, bf16[787264]{0:T(1024)(128)(2,1)S(1)} %convert_element_type.138, u32[]{:T(128)} %bitcast.2) | dynamic-update-slice | bytes 3149060
  43.8 0.9 copy-done.1
  44.8 0.2 fusion.40
  45.4 438.3 %all-reduce.8.cloned.1.call-done = bf16[12596224]{0:T(1024)(128)(2,1)} async-done(((bf16[12596224]{0:T(1024)(128)(2,1)}), bf16[12596224]{0:T(1024)(128)(2,1)}) %all-reduce.8.cloned.1.call-update) | async-done | bytes 25192464
  483.7 6.4 slice.135
  490.1 10.3 reshape.206
  500.4 0.7 slice_convert_fusion.8
  501.1 0.7 slice_convert_fusion.4
  501.8 3.9 convolution_add_fusion.1
  505.7 0.9 fusion.62
  506.6 0.9 slice-done.6
  507.5 2.3 slice.118
  509.8 2.5 convolution_convert_fusion
  512.3 0.2 copy.40
  512.4 0.2 copy.36
  512.6 0.2 copy.38
  512.9 0.2 copy.37
  513.2 0.4 fusion.64
  513.5 0.2 exponential_reduce_fusion
  513.7 0.3 fusion.41
  514.0 0.5 fusion.45
  514.5 0.4 fusion.8
  514.9 0.3 convolution_bitcast_fusion.1
  515.2 0.5 convolution_bitcast_fusion
  515.9 4.6 convert_bitcast_fusion.2
  520.5 0.5 fusion.12
  521.0 11.3 %fusion.61 = (bf16[4194304]{0:T(1024)(128)(2,1)}, bf16[4194304]{0:T(1024)(128)(2,1)}) fusion(bf16[12596224]{0:T(1024)(128)(2,1)} %all-reduce.8.cloned.1.call-done), kind=kLoop, calls=%fused_computation.130 | loop fusion | bytes 33554432 | tf_op jit(solution)/shard_map/slice | solution.py:45
  532.3 13.3 %slice.125 = bf16[4096,1024]{1,0:T(8,128)(2,1)} reshape(bf16[4194304]{0:T(1024)(128)(2,1)} %get-tuple-element.29) | data formatting | bytes 16777216 | tf_op jit(solution)/shard_map/slice | solution.py:45
  545.6 13.3 %reshape.209 = bf16[1024,4096]{1,0:T(8,128)(2,1)} reshape(bf16[4194304]{0:T(1024)(128)(2,1)} %get-tuple-element.28) | data formatting | bytes 16777216 | tf_op jit(solution)/shard_map/reshape | solution.py:45
  558.9 0.7 slice_convert_fusion.3
  559.6 4.9 convolution_add_fusion
  564.5 0.9 copy-done
  565.4 3.5 fusion.65
  568.9 2.9 fusion.43
  571.8 5.7 convert_bitcast_fusion.1
  577.5 4.6 convert_bitcast_fusion
  582.2 3.2 fusion.38
  585.3 1.9 copy.59
  587.3 3.0 constant_dynamic-update-slice_fusion.9
  590.3 0.8 convert_bitcast_fusion.3
  591.1 0.6 copy.60
  591.7 9.4 copy.61
  601.1 8.8 copy.62
  609.9 0.6 convert_dynamic-update-slice_fusion.1
  610.5 1.5 constant_dynamic-update-slice_fusion.8
  611.9 0.6 constant_dynamic-update-slice_fusion.7
  612.5 8.0 constant_dynamic-update-slice_fusion.6
  620.5 0.6 convert_dynamic-update-slice_fusion
  621.1 3.6 constant_dynamic-update-slice_fusion.5
  624.7 0.6 constant_dynamic-update-slice_fusion.4
  625.3 0.5 constant_dynamic-update-slice_fusion.3
  625.8 0.6 constant_dynamic-update-slice_fusion.2
  626.4 0.5 constant_dynamic-update-slice_fusion.1
  627.0 0.5 constant_dynamic-update-slice_fusion
  628.3 435.9 %all-reduce.10.cloned.1.call-done = bf16[12596224]{0:T(1024)(128)(2,1)} async-done(((bf16[12596224]{0:T(1024)(128)(2,1)}), bf16[12596224]{0:T(1024)(128)(2,1)}) %all-reduce.10.cloned.1.call-update) | async-done | bytes 25192464
  1064.2 3.4 dynamic-slice.2
  1067.7 2.1 fusion.34
  1069.8 5.3 convolution_add_fusion.3
  1075.1 1.2 fusion.11
  1076.3 42.7 %all-reduce.6.cloned.1.call-done = bf16[787264]{0:T(1024)(128)(2,1)} async-done(((bf16[787264]{0:T(1024)(128)(2,1)}), bf16[787264]{0:T(1024)(128)(2,1)}) %all-reduce.6.cloned.1.call-update) | async-done | bytes 1574544 | tf_op jit(solution)/shard_map/psum | solution.py:270
  1119.0 8.4 multiply_subtract_fusion
  (73 shorter events, 1.1 us)
Async XLA Ops:
  7.2 2.1 copy-start.12
  7.2 476.5 %all-reduce.8.cloned.1.call-start = ((), (), s32[]{:S(2)}) async-start(), calls=%async_computation.1 | async-start | bytes 50384896
  43.7 0.9 copy-start.1
  43.7 1.3 copy-start.11
  43.7 1.3 copy-start.3
  43.7 1020.5 %all-reduce.10.cloned.1.call-start = ((), (), s32[]{:S(2)}) async-start(), calls=%async_computation.2 | async-start | bytes 50384896
  505.7 1.8 slice-start.6
  509.8 2.8 copy-start.10
  515.9 4.6 copy-start.4
  515.9 4.6 copy-start.6
  559.6 5.8 copy-start
  559.6 9.2 slice-start
  565.4 3.5 slice-start.1
  571.8 10.4 copy-start.8
  571.8 10.4 slice-start.2
  571.8 13.5 %slice-start.7 = ((s8[6291456]{0:T(1024)(128)(4,1)}), s8[4194304]{0:T(1024)(128)(4,1)S(1)}, s32[]{:S(2)}) async-start(s8[6291456]{0:T(1024)(128)(4,1)} %bitcast.64), calls=%async_computation.10 | async-start | bytes 8388608
  577.5 4.7 slice-start.3
  577.5 4.7 copy-start.5
  577.5 4.7 copy-start.7
  577.5 7.8 slice-start.8
  612.5 8.6 slice-start.4
  612.5 8.6 slice-start.5
  627.5 440.1 %copy-start.9 = (f32[128,1024]{1,0:T(8,128)S(1)}, f32[128,1024]{1,0:T(8,128)}, u32[]{:S(2)}) copy-start(f32[128,1024]{1,0:T(8,128)} %copy-done.8) | copy-start | bytes 1572868
  627.6 491.5 %all-reduce.6.cloned.1.call-start = ((), (), s32[]{:S(2)}) async-start(), calls=%async_computation | async-start | bytes 3149824 | tf_op jit(solution)/shard_map/psum | solution.py:270
  1069.8 5.3 copy-start.2
Sparse Core Ops, SparseCore 0:
  43.9 439.7 all-reduce.7
  627.7 436.5 all-reduce.9
  1067.8 51.1 all-reduce.5
where the time goes:
time: 1140 us; the launch traced here: 1130 us
  waiting for transfers between devices  917 us (80%)
  local copies, waits for them, and re-layouts  140 us (12%)
  matrix products  45.2 us (4%)
  other arithmetic  16.2 us (1%)
  between operations  15.6 us (1%)
    unnamed x5, waiting for transfers between devices  874 us
    unnamed x61, local copies, waits for them, and re-layouts  79.8 us
    psum x1, waiting for transfers between devices, per_device(): grad_total = lax.psum(owner_part, 'rep').astype(jnp.float32)  42.7 us
    slice x6, local copies, waits for them, and re-layouts, unpack(): pieces.append(flat_vec[offset:offset + amount].reshape(extent))  34.2 us
    reshape x2, local copies, waits for them, and re-layouts, unpack(): pieces.append(flat_vec[offset:offset + amount].reshape(extent))  23.6 us
  transfers between devices with their start and end apart: 3, of which 3 were waited for; matrix products, arithmetic and copies ran while one was open for 1% of the time, Pallas kernels for 0%

commit v1 on v0

--- a/solution.py
+++ b/solution.py
@@ -267,7 +267,7 @@
         scatter_dimension=0,
         tiled=True,
     )
-    grad_total = lax.psum(owner_part, "rep").astype(jnp.float32)
+    grad_total = jnp.sum(lax.all_gather(owner_part, "rep"), axis=0).astype(jnp.float32)
     new_weights, first_new, second_new = adam_update(
         params, first_moment, second_moment, grad_total
     )

time: 1140 us -> 1260 us (1.11)
  local copies, waits for them, and re-layouts: 140 us -> 176 us
  other arithmetic: 16.2 us -> 48.6 us
  waiting for transfers between devices: 917 us -> 949 us
    unnamed x5 -> x6, waiting for transfers between devices: 874 us -> 949 us
    psum x1 -> x0, waiting for transfers between devices: 42.7 us -> none  [per_device(): grad_total = lax.psum(owner_part, 'rep').astype(jnp.float32)]
    reduce_sum x0 -> x1, other arithmetic: none -> 32.9 us  [per_device(): jnp.sum(lax.all_gather(owner_part, 'rep'), axis=0).astype(jnp.float32)]
    unnamed x61 -> x68, local copies, waits for them, and re-layouts: 79.8 us -> 108 us
where the time goes in v1:
time: 1260 us; the launch traced here: 1250 us
  waiting for transfers between devices  949 us (75%)
  local copies, waits for them, and re-layouts  176 us (14%)
  matrix products  56.2 us (4%)
  other arithmetic  48.6 us (4%)
  between operations  16.6 us (1%)
    unnamed x6, waiting for transfers between devices  949 us
    unnamed x68, local copies, waits for them, and re-layouts  108 us
    slice x6, local copies, waits for them, and re-layouts, unpack(): pieces.append(flat_vec[offset:offset + amount].reshape(extent))  34.2 us
    reduce_sum x1, other arithmetic, per_device(): jnp.sum(lax.all_gather(owner_part, 'rep'), axis=0).astype(jnp.float32)  32.9 us
  transfers between devices with their start and end apart: 3, of which 3 were waited for; matrix products, arithmetic and copies ran while one was open for 1% of the time, Pallas kernels for 0%

profile of v1, /device:TPU:0, one launch (start us, length us, event | category | flops | bytes accessed | tf_op | source)
XLA Modules:
  0.0 1246.4 jit_solution(8914739560040263521)
XLA Ops:
  7.2 2.0 convert_element_type.140
  9.3 0.6 fusion.63
  10.6 8.4 broadcast.159
  19.0 24.7 %dynamic-update-slice = bf16[12596224]{0:T(1024)(128)(2,1)} dynamic-update-slice(bf16[12596224]{0:T(1024)(128)(2,1)} %broadcast.159, bf16[787264]{0:T(1024)(128)(2,1)S(1)} %convert_element_type.140, u32[]{:T(128)} %bitcast.2) | dynamic-update-slice | bytes 3149060
  43.7 0.9 copy-done.1
  45.3 438.3 %all-reduce.7.cloned.1.call-done = bf16[12596224]{0:T(1024)(128)(2,1)} async-done(((bf16[12596224]{0:T(1024)(128)(2,1)}), bf16[12596224]{0:T(1024)(128)(2,1)}) %all-reduce.7.cloned.1.call-update) | async-done | bytes 25192464
  483.6 6.4 slice.135
  490.0 10.3 reshape.206
  500.3 0.7 slice_convert_fusion.8
  501.0 0.7 slice_convert_fusion.4
  501.7 3.9 convolution_add_fusion.1
  505.6 0.9 fusion.62
  506.5 0.9 slice-done.6
  507.4 2.3 slice.118
  509.7 2.5 convolution_convert_fusion
  513.0 0.4 fusion.64
  513.6 0.3 fusion.41
  513.9 0.5 fusion.45
  514.4 0.4 fusion.8
  514.8 0.3 convolution_bitcast_fusion.1
  515.1 0.5 convolution_bitcast_fusion
  515.8 4.5 convert_bitcast_fusion.2
  520.4 0.5 fusion.12
  520.8 11.3 fusion.61
  532.2 13.3 %slice.125 = bf16[4096,1024]{1,0:T(8,128)(2,1)} reshape(bf16[4194304]{0:T(1024)(128)(2,1)} %get-tuple-element.29) | data formatting | bytes 16777216 | tf_op jit(solution)/shard_map/slice | solution.py:45
  545.5 13.3 %reshape.209 = bf16[1024,4096]{1,0:T(8,128)(2,1)} reshape(bf16[4194304]{0:T(1024)(128)(2,1)} %get-tuple-element.28) | data formatting | bytes 16777216 | tf_op jit(solution)/shard_map/reshape | solution.py:45
  558.8 0.7 slice_convert_fusion.3
  559.5 4.9 convolution_add_fusion
  564.4 0.9 copy-done
  565.2 14.1 %fusion.65 = (bf16[4096]{0:T(1024)(128)(2,1)S(1)}, bf16[128,4096]{1,0:T(8,128)(2,1)S(1)}) fusion(f32[128,4096]{1,0:T(8,128)S(1)} %convolution_add_fusion, bf16[4096,1024]{1,0:T(8,128)(2,1)S(1)} %copy-done, bf16[128,1024]{1,0:T(8,128)(2,1)S(1)} %copy-done.4, pred[128]{0:T(512)(128)(4,1)S(1)} %broadcast_compare_fusion), kind=kOutput, calls=%fused_computation.134 | convolution fusion | flops 1079635968 | bytes 11804800 | tf_op jit(solution)/shard_map/dot_general | solution.py:183
  579.4 2.9 fusion.43
  582.3 5.7 convert_bitcast_fusion.1
  588.0 4.7 convert_bitcast_fusion
  592.7 3.2 fusion.38
  596.0 1.9 copy.68
  597.9 3.0 constant_dynamic-update-slice_fusion.9
  600.9 0.8 convert_bitcast_fusion.3
  601.6 0.6 copy.69
  602.3 9.4 copy.70
  611.7 8.8 copy.71
  620.5 0.6 convert_dynamic-update-slice_fusion.1
  621.1 1.5 constant_dynamic-update-slice_fusion.8
  622.5 0.6 constant_dynamic-update-slice_fusion.7
  623.1 8.1 constant_dynamic-update-slice_fusion.6
  631.2 0.6 convert_dynamic-update-slice_fusion
  631.8 3.6 constant_dynamic-update-slice_fusion.5
  635.4 0.6 constant_dynamic-update-slice_fusion.4
  636.0 0.5 constant_dynamic-update-slice_fusion.3
  636.5 0.6 constant_dynamic-update-slice_fusion.2
  637.1 0.5 constant_dynamic-update-slice_fusion.1
  637.7 0.6 constant_dynamic-update-slice_fusion
  638.3 0.6 copy-done.14
  638.9 0.6 dynamic-slice.1
  640.8 434.2 %all-reduce.11.cloned.1.call-done = bf16[12596224]{0:T(1024)(128)(2,1)} async-done(((bf16[12596224]{0:T(1024)(128)(2,1)}), bf16[12596224]{0:T(1024)(128)(2,1)}) %all-reduce.11.cloned.1.call-update) | async-done | bytes 25192464
  1075.0 3.4 dynamic-slice.3
  1078.4 1.8 broadcast.160
  1080.1 25.3 %dynamic-update-slice.1 = bf16[1574528]{0:T(1024)(128)(2,1)} dynamic-update-slice(bf16[1574528]{0:T(1024)(128)(2,1)} %broadcast.160, bf16[787264]{0:T(1024)(128)(2,1)} %dynamic-slice.3, u32[]{:T(128)} %bitcast.19) | dynamic-update-slice | bytes 3149060
  1105.6 2.1 fusion.34
  1107.7 5.6 convolution_add_fusion.3
  1113.3 1.2 fusion.11
  1114.5 76.6 %all-reduce.9.cloned.1.call-done = bf16[1574528]{0:T(1024)(128)(2,1)} async-done(((bf16[1574528]{0:T(1024)(128)(2,1)}), bf16[1574528]{0:T(1024)(128)(2,1)}) %all-reduce.9.cloned.1.call-update) | async-done | bytes 3149072
  1191.1 7.6 reshape.214
  1198.7 32.9 %reduce_sum.163 = bf16[787264]{0:T(1024)(128)(2,1)} reduce(bf16[2,787264]{1,0:T(2,128)(2,1)} %reshape.214, bf16[]{:T(256)} %constant.48.clone.1), dimensions={0}, to_apply=%region_16.17 | reduce | flops 787264 | bytes 4723586 | tf_op jit(solution)/shard_map/reduce_sum | solution.py:270
  1231.6 7.9 multiply_subtract_fusion
  (82 shorter events, 2.2 us)
Async XLA Ops:
  7.2 2.1 copy-start.13
  7.2 476.4 %all-reduce.7.cloned.1.call-start = ((), (), s32[]{:S(2)}) async-start(), calls=%async_computation | async-start | bytes 50384896
  43.6 0.9 copy-start.1
  43.6 1.3 copy-start.12
  43.7 1.3 copy-start.4
  43.7 1031.3 %all-reduce.11.cloned.1.call-start = ((), (), s32[]{:S(2)}) async-start(), calls=%async_computation.2 | async-start | bytes 50384896
  505.6 1.8 slice-start.6
  509.7 2.8 copy-start.11
  515.8 4.6 copy-start.5
  515.8 4.6 copy-start.7
  559.5 5.8 copy-start
  559.5 19.9 %slice-start = ((s8[8388608]{0:T(1024)(128)(4,1)}), s8[4194304]{0:T(1024)(128)(4,1)S(1)}, s32[]{:S(2)}) async-start(s8[8388608]{0:T(1024)(128)(4,1)} %bitcast.57), calls=%async_computation.3 | async-start | bytes 8388608
  565.2 14.1 %slice-start.1 = ((s8[8388608]{0:T(1024)(128)(4,1)}), s8[4194304]{0:T(1024)(128)(4,1)S(1)}, s32[]{:S(2)}) async-start(s8[8388608]{0:T(1024)(128)(4,1)} %bitcast.57), calls=%async_computation.4 | async-start | bytes 8388608
  582.3 10.5 copy-start.9
  582.3 10.4 slice-start.2
  582.3 13.7 %slice-start.7 = ((s8[6291456]{0:T(1024)(128)(4,1)}), s8[4194304]{0:T(1024)(128)(4,1)S(1)}, s32[]{:S(2)}) async-start(s8[6291456]{0:T(1024)(128)(4,1)} %bitcast.65), calls=%async_computation.10 | async-start | bytes 8388608
  588.0 4.7 slice-start.3
  588.0 4.7 copy-start.6
  588.0 4.7 copy-start.8
  588.0 7.9 slice-start.8
  623.1 8.7 slice-start.4
  623.1 8.7 slice-start.5
  638.2 0.7 copy-start.14
  638.3 552.8 %all-reduce.9.cloned.1.call-start = ((), (), s32[]{:S(2)}) async-start(), calls=%async_computation.1 | async-start | bytes 6299648
  1080.1 25.4 %copy-start.10 = (f32[128,1024]{1,0:T(8,128)S(1)}, f32[128,1024]{1,0:T(8,128)}, u32[]{:S(2)}) copy-start(f32[128,1024]{1,0:T(8,128)} %copy-done.9) | copy-start | bytes 1572868
  1107.7 5.6 copy-start.2
  1198.7 32.9 %copy-start.3 = (f32[787264]{0:T(1024)S(1)}, f32[787264]{0:T(1024)}, u32[]{:S(2)}) copy-start(f32[787264]{0:T(1024)} %param.9) | copy-start | bytes 9447172
Sparse Core Ops, SparseCore 0:
  43.8 439.7 all-reduce.6
  638.4 436.5 all-reduce.10
  1105.6 85.4 all-reduce.8
